TPU v7x, 128 devices: a whole 4x4x4 slice. The times are simulated.
128 devices in a mesh: ctx: 64 (over z, y, x_lo, core), tp: 2 (over x_hi).
Axes of the slice: x: 4 (x_hi: 2, x_lo: 2; x = x_hi * 2 + x_lo), y: 4, z: 4, core: 2. Of those that a mesh axis runs over, the one named last changes fastest.
Arguments:
- queries: bfloat16 [32768, 4096], P('ctx', 'tp'), may hold values from -0.19921875 to 0.19921875
- keys: bfloat16 [32768, 4096], P('ctx', 'tp'), may hold values from -0.19921875 to 0.19921875
- values: bfloat16 [32768, 4096], P('ctx', 'tp'), may hold values from -0.19921875 to 0.19921875
- cotangent: bfloat16 [32768, 2048], P('ctx', 'tp'), may hold values from -6 to 6
- out_weight: bfloat16 [4096, 2048], P('tp'), may hold values from -0.125 to 0.125
- memory: float32 [32, 128, 128], P('tp'), may hold values from -0.6 to 0.6
Outputs:
- query_grad: bfloat16 [32768, 4096], P('ctx', 'tp')
- key_grad: bfloat16 [32768, 4096], P('ctx', 'tp')
- value_grad: bfloat16 [32768, 4096], P('ctx', 'tp')
- weight_grad: float32 [4096, 2048], P(('tp', 'ctx'))
All inputs are finite; a program needn't handle non-finite values.
Results may differ from a plain program's by a relative error of at most 0.0058.
Values may be sent and summed in bfloat16 or wider, within the bound.
A program may use at most 320 MiB of HBM per device.

v0:
```python
import jax
import jax.numpy as jnp
from jax import lax
from jax.sharding import PartitionSpec as P


def carried_in(value, axis, combine, identity, reverse):
    peers, index = (lax.axis_size(axis), lax.axis_index(axis))
    everything = lax.all_gather(value, axis)
    start = jnp.broadcast_to(jnp.asarray(identity, value.dtype), value.shape)

    def lap(k, before):
        at = peers - 1 - k if reverse else k
        reached = at > index if reverse else at < index
        new = combine(before, everything[at])
        return jnp.where(reached, new, before)

    return lax.fori_loop(0, peers, lap, start)


def add_pair(earlier, later):
    return earlier + later


def local(queries, keys, values, cotangent, out_weight, memory):
    tok_rows, col_width = queries.shape
    heads = memory.shape[0]
    head_size = memory.shape[1]
    full_cot = lax.all_gather(cotangent, "tp", axis=1, tiled=True)
    out_grad = lax.dot_general(
        full_cot, out_weight, (((1,), (1,)), ((), ())), preferred_element_type=jnp.float32
    ).astype(jnp.bfloat16)
    query_heads = queries.reshape(tok_rows, heads, head_size)
    key_heads = keys.reshape(tok_rows, heads, head_size)
    value_heads = values.reshape(tok_rows, heads, head_size)
    grad_heads = out_grad.reshape(tok_rows, heads, head_size)
    kv_sum = jnp.einsum("the,thf->hef", key_heads, value_heads, preferred_element_type=jnp.float32)
    qd_sum = jnp.einsum("the,thf->hef", query_heads, grad_heads, preferred_element_type=jnp.float32)
    zeros = jnp.zeros_like(kv_sum)
    before = carried_in(kv_sum, "ctx", add_pair, zeros, False)
    after = carried_in(qd_sum, "ctx", add_pair, zeros, True)
    state = (memory + before).astype(jnp.bfloat16)
    adjoint = after.astype(jnp.bfloat16)
    causal = lax.broadcasted_iota(jnp.int32, (tok_rows, tok_rows), 0) >= lax.broadcasted_iota(
        jnp.int32, (tok_rows, tok_rows), 1
    )
    scores = jnp.einsum("the,she->hts", query_heads, key_heads, preferred_element_type=jnp.float32)
    scores = jnp.where(causal[None], scores, 0.0).astype(jnp.bfloat16)
    dscores = jnp.einsum(
        "thf,shf->hts", grad_heads, value_heads, preferred_element_type=jnp.float32
    )
    dscores = jnp.where(causal[None], dscores, 0.0).astype(jnp.bfloat16)
    attended = jnp.einsum(
        "the,hef->thf", query_heads, state, preferred_element_type=jnp.float32
    ) + jnp.einsum("hts,shf->thf", scores, value_heads, preferred_element_type=jnp.float32)
    attended = attended.astype(jnp.bfloat16).reshape(tok_rows, col_width)
    query_g = jnp.einsum(
        "thf,hef->the", grad_heads, state, preferred_element_type=jnp.float32
    ) + jnp.einsum("hts,she->the", dscores, key_heads, preferred_element_type=jnp.float32)
    key_g = jnp.einsum(
        "shf,hef->she", value_heads, adjoint, preferred_element_type=jnp.float32
    ) + jnp.einsum("hts,the->she", dscores, query_heads, preferred_element_type=jnp.float32)
    value_g = jnp.einsum(
        "she,hef->shf", key_heads, adjoint, preferred_element_type=jnp.float32
    ) + jnp.einsum("hts,thf->shf", scores, grad_heads, preferred_element_type=jnp.float32)
    weight_grad = lax.psum_scatter(
        lax.dot_general(
            attended, full_cot, (((0,), (0,)), ((), ())), preferred_element_type=jnp.float32
        ),
        "ctx",
        scatter_dimension=0,
        tiled=True,
    )
    return (
        query_g.astype(jnp.bfloat16).reshape(tok_rows, col_width),
        key_g.astype(jnp.bfloat16).reshape(tok_rows, col_width),
        value_g.astype(jnp.bfloat16).reshape(tok_rows, col_width),
        weight_grad,
    )


def solution(mesh):
    in_specs = (
        P("ctx", "tp"),
        P("ctx", "tp"),
        P("ctx", "tp"),
        P("ctx", "tp"),
        P("tp", None),
        P("tp", None, None),
    )
    out_specs = (P("ctx", "tp"), P("ctx", "tp"), P("ctx", "tp"), P(("tp", "ctx"), None))
    return jax.shard_map(local, mesh=mesh, in_specs=in_specs, out_specs=out_specs, check_vma=False)
```

profile of v0, /device:TPU:1, one launch (start us, length us, event | category | flops | bytes accessed | tf_op | source)
XLA Modules:
  0.0 1100.7 jit_solution(14394564023939348940)
XLA Ops:
  8.0 3.9 copy.56
  11.9 4.0 fusion.10
  15.9 33.9 %all-gather.6.cloned.1.call-done = bf16[512,2048]{1,0:T(8,128)(2,1)} async-done(((bf16[512,1024]{1,0:T(8,128)(2,1)}), bf16[512,2048]{1,0:T(8,128)(2,1)}) %all-gather.6.cloned.1.call-update) | async-done | bytes 2097168 | tf_op jit(solution)/shard_map/all_gather | solution.py:29
  49.8 9.9 convolution_convert_fusion
  59.7 4.0 copy.57
  63.7 2.3 fusion.15
  67.6 7.2 select_convert_fusion
  74.8 338.9 %all-gather.8.cloned.1.call-done = f32[1024,128,128]{2,1,0:T(8,128)} async-done(((f32[16,128,128]{2,1,0:T(8,128)}), f32[1024,128,128]{2,1,0:T(8,128)}) %all-gather.8.cloned.1.call-update) | async-done | bytes 67108880 | tf_op jit(solution)/shard_map/all_gather | solution.py:9
  413.7 104.7 %while.30 = (s32[]{:T(128)}, f32[16,128,128]{2,1,0:T(8,128)S(1)}, s32[]{:T(128)}, f32[64,16,128,128]{3,2,1,0:T(8,128)}, s32[]{:T(128)}, /*index=5*/s32[]{:T(128)}) while((s32[]{:T(128)}, f32[16,128,128]{2,1,0:T(8,128)S(1)}, s32[]{:T(128)}, f32[64,16,128,128]{3,2,1,0:T(8,128)}, s32[]{:T(128)}, /*index=5*/s32[]{:T(128)}) %tuple.74), condition=%wide.region_1.2_spmd.clone, body=%wide.region_0.1_spmd.clone.sunk | while | flops 786436 | bytes 3145829 | solution.py:18
  425.0 1.8 add_select_fusion.4
  430.0 1.7 add_select_fusion.4
  433.3 1.6 add_select_fusion.4
  436.6 1.6 add_select_fusion.4
  441.4 1.6 add_select_fusion.4
  444.7 1.6 add_select_fusion.4
  448.0 1.6 add_select_fusion.4
  449.6 1.7 add_select_fusion.4
  461.1 1.7 add_select_fusion.4
  469.2 1.7 add_select_fusion.4
  472.6 1.6 add_select_fusion.4
  475.8 1.6 add_select_fusion.4
  480.7 1.7 add_select_fusion.4
  484.0 1.6 add_select_fusion.4
  487.3 1.6 add_select_fusion.4
  488.9 1.7 add_select_fusion.4
  492.2 1.6 add_select_fusion.4
  495.5 1.6 add_select_fusion.4
  500.3 1.7 add_select_fusion.4
  503.7 1.6 add_select_fusion.4
  508.5 1.7 add_select_fusion.4
  511.9 1.6 add_select_fusion.4
  515.1 1.6 add_select_fusion.4
  522.2 7.7 fusion
  529.9 12.7 %fusion.30 = f32[2048,2048]{1,0:T(8,128)} fusion(bf16[512,2048]{0,1:T(8,128)(2,1)} %bitcast.113, bf16[512,2048]{1,0:T(8,128)(2,1)} %all-gather.6.cloned.1.call-done), kind=kOutput, calls=%fused_computation.39 | convolution fusion | flops 4294967296 | bytes 20971520 | tf_op jit(solution)/shard_map/dot_general | solution.py:67
  542.6 8.1 select_convert_fusion.1
  550.7 2.7 fusion.29
  553.4 9.1 fusion.2
  562.5 3.9 copy.51
  566.4 211.4 %all-gather.10.cloned.1.call-done = f32[1024,128,128]{2,1,0:T(8,128)} async-done(((f32[16,128,128]{2,1,0:T(8,128)}), f32[1024,128,128]{2,1,0:T(8,128)}) %all-gather.10.cloned.1.call-update) | async-done | bytes 67108880 | tf_op jit(solution)/shard_map/all_gather | solution.py:9
  777.8 104.1 %while.31 = (s32[]{:T(128)}, f32[16,128,128]{2,1,0:T(8,128)S(1)}, s32[]{:T(128)}, f32[64,16,128,128]{3,2,1,0:T(8,128)}, s32[]{:T(128)}, /*index=5*/s32[]{:T(128)}, s32[]{:T(128)}, s32[]{:T(128)}) while((s32[]{:T(128)}, f32[16,128,128]{2,1,0:T(8,128)S(1)}, s32[]{:T(128)}, f32[64,16,128,128]{3,2,1,0:T(8,128)}, s32[]{:T(128)}, ...), condition=%wide.region_3.4_spmd.clone, body=%wide.region_2.3_spmd.clone.sunk | while | flops 786440 | bytes 3145891 | solution.py:18
  789.2 1.7 add_select_fusion.5
  881.9 2.3 fusion.27
  884.2 6.2 fusion.1
  890.4 3.9 copy.52
  894.3 2.5 fusion.13
  896.9 6.3 add_convert_fusion
  903.1 3.9 copy.53
  907.0 187.2 %reduce-scatter.2.cloned.1.call-done = f32[32,2048]{1,0:T(8,128)} async-done(((f32[2048,2048]{1,0:T(8,128)}), f32[32,2048]{1,0:T(8,128)}) %reduce-scatter.2.cloned.1.call-update) | async-done | bytes 262160 | tf_op jit(solution)/shard_map/reduce_scatter | solution.py:66
  (132 shorter events, 172.0 us)
Async XLA Ops:
  7.2 56.5 %copy-start = (bf16[512,2048]{1,0:T(8,128)(2,1)S(1)}, bf16[512,2048]{1,0:T(8,128)(2,1)}, u32[]{:S(2)}) copy-start(bf16[512,2048]{1,0:T(8,128)(2,1)} %param.10) | copy-start | bytes 6291460
  7.2 42.6 %all-gather.6.cloned.1.call-start = ((), (), s32[]{:S(2)}) async-start(), calls=%async_computation.1 | async-start | bytes 3145728 | tf_op jit(solution)/shard_map/all_gather | solution.py:29
  7.9 405.8 %all-gather.8.cloned.1.call-start = ((), (), s32[]{:S(2)}) async-start(), calls=%async_computation.3 | async-start | bytes 68157440 | tf_op jit(solution)/shard_map/all_gather | solution.py:9
  15.9 761.9 %all-gather.10.cloned.1.call-start = ((), (), s32[]{:S(2)}) async-start(), calls=%async_computation.4 | async-start | bytes 68157440 | tf_op jit(solution)/shard_map/all_gather | solution.py:9
  67.4 1026.8 %reduce-scatter.2.cloned.1.call-start = ((), (), s32[]{:S(2)}) async-start(), calls=%async_computation.2 | async-start | bytes 17039360 | tf_op jit(solution)/shard_map/reduce_scatter | solution.py:66
  519.7 0.8 copy-start.5
  520.5 1.6 copy-start.1
  542.6 8.1 copy-start.2
  542.6 8.1 copy-start.6
  550.7 2.7 copy-start.4
  894.3 2.5 copy-start.3
Sparse Core Ops, SparseCore 0:
  9.6 40.1 all-gather.5
  52.1 361.5 all-gather.7
  415.4 362.3 all-gather.9
  780.7 313.4 reduce-scatter.1
where the time goes:
time: 1110 us; the launch traced here: 1100 us
  waiting for transfers between devices  772 us (70%)
  other arithmetic  207 us (19%)
  matrix products  81.7 us (7%)
  local copies, waits for them, and re-layouts  22.7 us (2%)
  between operations  13.9 us (1%)
    all_gather x2, waiting for transfers between devices, carried_in(): everything = lax.all_gather(value, axis)  550 us
    select_n x128, other arithmetic, lap(): return jnp.where(reached, new, before)  205 us
    reduce_scatter x1, waiting for transfers between devices, local(): lax.psum_scatter(lax.dot_general(attended, full_cot, (((0,), (0,)), ((),...  187 us
    all_gather x1, waiting for transfers between devices, local(): full_cot = lax.all_gather(cotangent, 'tp', axis=1, tiled=True)  33.9 us
  transfers between devices with their start and end apart: 4, of which 4 were waited for; matrix products, arithmetic and copies ran while one was open for 28% of the time, Pallas kernels for 0%

commit v1 on v0

v1 whole, which is shorter than its diff:
```python
import jax
import jax.numpy as jnp
from jax import lax
from jax.experimental import pallas as pl
from jax.experimental.pallas import tpu as pltpu
from jax.sharding import PartitionSpec as P

MESH = pl.DeviceIdType.MESH
BF = jnp.bfloat16
F32 = jnp.float32
VM = pltpu.VMEM
DMA = pltpu.SemaphoreType.DMA


def nn(a, b):
    return lax.dot_general(a, b, (((1,), (0,)), ((), ())), preferred_element_type=F32)


def nt(a, b):
    return lax.dot_general(a, b, (((1,), (1,)), ((), ())), preferred_element_type=F32)


def tn(a, b):
    return lax.dot_general(a, b, (((0,), (0,)), ((), ())), preferred_element_type=F32)


def head(h):
    return pl.ds(pl.multiple_of(h * 128, 128), 128)


def loop(lo, hi, body):
    def step(i, carry):
        body(i)
        return carry

    lax.fori_loop(lo, hi, step, 0)


class Place:
    def __init__(self):
        self.me = lax.axis_index("ctx")
        self.tp = lax.axis_index("tp")
        self.p = self.me % 4
        self.core = self.me % 2
        self.zy = self.me // 4
        self.z = self.me // 16
        self.y = self.zy % 4
        self.base = self.me - self.p

    def group(self, p):
        return (self.base + p, self.tp)

    def plane(self, zy):
        return (zy * 4 + self.p, self.tp)

    def along_y(self, y):
        return (self.me + (y - self.y) * 4, self.tp)

    def along_z(self, z):
        return (self.me + (z - self.z) * 16, self.tp)


def remote(src, dst, send, recv, device):
    return pltpu.make_async_remote_copy(
        src_ref=src, dst_ref=dst, send_sem=send, recv_sem=recv, device_id=device, device_id_type=MESH
    )


class Scan:
    def __init__(self, at, refs, reverse):
        self.at, self.reverse = at, reverse
        (self.s, self.a, self.t, self.b, self.pre, self.c, self.d, self.st, self.ga, self.gd, self.pb, self.pc) = refs

    def up_group(self, k):
        q = (self.at.p + k) % 4
        return remote(
            self.s.at[pl.ds(q * 4, 4)], self.a.at[self.at.p], self.ga.at[0, k - 1], self.ga.at[1, k - 1], self.at.group(q)
        )

    def send_up_group(self):
        for k in range(1, 4):
            self.up_group(k).start()
        self.a[self.at.p] = self.s[pl.ds(self.at.p * 4, 4)]

    def up_plane(self, k):
        j = (self.at.zy + k) % 16
        return remote(self.t.at[j], self.b.at[self.at.zy], self.pb.at[0], self.pb.at[1], self.at.plane(j))

    def send_up_plane(self):
        for k in range(1, 4):
            self.up_group(k).wait()
        for h in range(4):
            total = self.a[0, h].astype(F32)
            for q in range(1, 4):
                total = total + self.a[q, h].astype(F32)
            self.t[pl.ds(4 * h, 4)] = total.reshape(4, 32, 128)
        loop(1, 16, lambda k: self.up_plane(k).start())
        self.b[self.at.zy] = self.t[self.at.zy]

    def down_plane(self, k):
        j = (self.at.zy + k) % 16
        return remote(self.pre.at[j], self.c.at[self.at.zy], self.pc.at[0], self.pc.at[1], self.at.plane(j))

    def wait_all(self, src, dst, sems):
        pltpu.make_async_copy(src.at[pl.ds(0, 15)], src.at[pl.ds(0, 15)], sems.at[0]).wait()
        pltpu.make_async_copy(dst.at[pl.ds(0, 15)], dst.at[pl.ds(0, 15)], sems.at[1]).wait()

    def send_down_plane(self):
        self.wait_all(self.t, self.b, self.pb)
        run = jnp.zeros((32, 128), F32)
        for i in reversed(range(16)) if self.reverse else range(16):
            self.pre[i] = run
            run = run + self.b[i]
        loop(1, 16, lambda k: self.down_plane(k).start())
        self.c[self.at.zy] = self.pre[self.at.zy]

    def down_group(self, k):
        q = (self.at.p + k) % 4
        return remote(
            self.d.at[q], self.st.at[pl.ds(self.at.p * 4, 4)], self.gd.at[0, k - 1], self.gd.at[1, k - 1], self.at.group(q)
        )

    def send_down_group(self, memory):
        self.wait_all(self.pre, self.c, self.pc)
        for h in range(4):
            run = self.c[pl.ds(4 * h, 4)].reshape(128, 128)
            if memory is not None:
                run = run + memory[h]
            for q in reversed(range(4)) if self.reverse else range(4):
                self.d[q, h] = run.astype(BF)
                run = run + self.a[q, h].astype(F32)
        for k in range(1, 4):
            self.down_group(k).start()
        self.st[pl.ds(self.at.p * 4, 4)] = self.d[self.at.p]

    def finish(self):
        for k in range(1, 4):
            self.down_group(k).wait()


class Ring:
    def __init__(self, src, land, sems, pos, device):
        self.src, self.land, self.sems, self.pos = src, land, sems, pos
        self.quarters = [pos, (pos + 1) % 4, (pos + 2) % 4, (pos + 3) % 4]
        self.device = device

    def copy(self, way, slot):
        near = self.quarters[1] if way == 0 else self.quarters[3]
        if slot == 0:
            src = self.src.at[self.quarters[2], way]
        elif slot == 1:
            src = self.src.at[near, 1 - way]
        else:
            src = self.src.at[near, way]
        return remote(
            src, self.land.at[way, slot], self.sems.at[0, way, slot], self.sems.at[1, way, slot], self.device(near)
        )

    def send_far(self):
        self.copy(0, 0).start()
        self.copy(1, 0).start()

    def send_near(self, way):
        self.copy(way, 1).start()

    def relay(self, way):
        near = self.quarters[1] if way == 0 else self.quarters[3]
        self.copy(way, 0).wait()
        self.src[near, way] = (self.src[near, way].astype(F32) + self.land[way, 0].astype(F32)).astype(BF)
        self.copy(way, 2).start()

    def result(self, half):
        own = self.src[self.pos, half].astype(F32)
        for way in range(2):
            slot = 2 if way == half else 1
            own = own + self.land[way, slot].astype(F32)
        return own

    def wait_results(self):
        for way in range(2):
            self.copy(way, 1).wait()
            self.copy(way, 2).wait()


def kernel(
    q_hbm, k_hbm, v_hbm, cot_hbm, w_hbm, mem_hbm,
    qg_hbm, kg_hbm, vg_hbm, wg_hbm,
    q, k, v, w, cot, pcot, mem, gacc, g, intra,
    kv_refs, qd_refs,
    att, pa, pb, land_a1, land_b1, s1a, s1b, land_a2, land_b2, fin, fin_land,
    qg, kg, vg, wg,
    in_sem, out_sem, tp_sem, pc_sem, at_sem, ring_sem, fin_sem,
):
    at = Place()
    me, tp, core = at.me, at.tp, at.core
    peer_core = (at.base + (at.p + 1 - 2 * core), tp)
    peer_tp = (me, 1 - tp)

    loads = [
        pltpu.make_async_copy(k_hbm, k, in_sem.at[0]),
        pltpu.make_async_copy(v_hbm, v, in_sem.at[1]),
        pltpu.make_async_copy(q_hbm, q, in_sem.at[2]),
        pltpu.make_async_copy(cot_hbm, cot.at[tp], in_sem.at[3]),
        pltpu.make_async_copy(w_hbm.at[:, pl.ds(0, 1024)], w.at[0], in_sem.at[4]),
        pltpu.make_async_copy(w_hbm.at[:, pl.ds(1024, 1024)], w.at[1], in_sem.at[5]),
        pltpu.make_async_copy(mem_hbm.at[pl.ds(at.p * 4, 4)], mem, in_sem.at[6]),
    ]
    for load in loads:
        load.start()

    barrier = pltpu.get_barrier_semaphore()

    def signal(device):
        pl.semaphore_signal(barrier, inc=1, device_id=device, device_id_type=MESH)

    signal(peer_tp)
    for i in range(1, 4):
        signal(at.group((at.p + i) % 4))
    loop(1, 16, lambda i: signal(at.plane((at.zy + i) % 16)))
    pl.semaphore_wait(barrier, 19)

    cot_copy = remote(cot_hbm, cot.at[tp], tp_sem.at[0], tp_sem.at[1], peer_tp)
    cot_copy.start()

    kv = Scan(at, kv_refs, False)
    qd = Scan(at, qd_refs, True)

    loads[0].wait()
    loads[1].wait()

    def kv_sum(h):
        kv.s[h] = tn(k[:, head(h)], v[:, head(h)]).astype(BF)

    loop(0, 16, kv_sum)
    kv.send_up_group()

    loads[2].wait()
    row = lax.broadcasted_iota(jnp.int32, (256, 256), 0)
    col = lax.broadcasted_iota(jnp.int32, (256, 256), 1)

    def lower(x):
        return jnp.where(row >= col, x, 0.0).astype(BF)

    def upper(x):
        return jnp.where(row <= col, x, 0.0).astype(BF)

    top, low = pl.ds(0, 256), pl.ds(256, 256)

    def causal(a, b, c, h):
        hs = head(h)
        a0, a1, b0, b1, c0, c1 = a[top, hs], a[low, hs], b[top, hs], b[low, hs], c[top, hs], c[low, hs]
        first = nn(lower(nt(a0, b0)), c0)
        second = nn(nt(a1, b0).astype(BF), c0) + nn(lower(nt(a1, b1)), c1)
        return first, second

    def anti(b, a, c, h):
        hs = head(h)
        a0, a1, b0, b1, c0, c1 = a[top, hs], a[low, hs], b[top, hs], b[low, hs], c[top, hs], c[low, hs]
        first = nn(upper(nt(b0, a0)), c0) + nn(nt(b0, a1).astype(BF), c1)
        second = nn(upper(nt(b1, a1)), c1)
        return first, second

    def scored(h):
        first, second = causal(q, k, v, h)
        intra[h, top] = first
        intra[h, low] = second

    loop(0, 8, scored)
    kv.send_up_plane()
    loop(8, 16, scored)

    loads[3].wait()
    loads[4].wait()
    loads[5].wait()

    def wrows(n):
        return pl.ds(pl.multiple_of(n * 256, 256), 256)

    def grad_own(n):
        gacc[:, wrows(n)] = nt(cot[tp], w[tp, wrows(n), :])

    loop(0, 4, grad_own)
    kv.send_down_plane()
    loop(4, 8, grad_own)

    loads[6].wait()
    kv.send_down_group(mem)

    cot_copy.wait()
    pcot_copy = remote(cot.at[1 - core], pcot, pc_sem.at[0], pc_sem.at[1], peer_core)
    pcot_copy.start()

    def grad_other(n):
        g[:, wrows(n)] = (gacc[:, wrows(n)] + nt(cot[1 - tp], w[1 - tp, wrows(n), :])).astype(BF)

    loop(0, 8, grad_other)

    def qd_sum(h):
        qd.s[h] = tn(q[:, head(h)], g[:, head(h)]).astype(BF)

    loop(0, 16, qd_sum)
    qd.send_up_group()

    kv.finish()

    def attend(h):
        a = intra[h] + nn(q[:, head(h)], kv.st[h])
        att[0, h // 4, h % 4] = a.T.astype(BF)

    att_copies = []
    for i in range(4):
        loop(4 * i, 4 * i + 4, attend)
        att_copies.append(remote(att.at[0, i], att.at[1, i], at_sem.at[0, i], at_sem.at[1, i], peer_core))
        att_copies[i].start()

    qd.send_up_plane()

    pcot_copy.wait()
    for copy in att_copies:
        copy.wait()

    y, z = at.y, at.z
    ring_a1 = Ring(pa, land_a1, ring_sem.at[0], y, at.along_y)
    ring_b1 = Ring(pb, land_b1, ring_sem.at[1], z, at.along_z)
    ring_a2 = Ring(s1a, land_a2, ring_sem.at[2], z, at.along_z)
    ring_b2 = Ring(s1b, land_b2, ring_sem.at[3], y, at.along_y)

    def part_a(i):
        yq = ring_a1.quarters[i]
        cols = pl.ds(0, 512)
        r = nn(att[0, :, yq].reshape(512, 512), cot[core, :, cols])
        r = r + nn(att[1, :, yq].reshape(512, 512), pcot[:, cols])
        pa[yq] = r.astype(BF).reshape(2, 2, 128, 512)

    def part_b(i):
        zq = ring_b1.quarters[i]
        cols = pl.ds(512, 512)
        r = nn(att[0, zq].reshape(512, 512), cot[core, :, cols])
        r = r + nn(att[1, zq].reshape(512, 512), pcot[:, cols])
        pb[zq] = r.astype(BF).reshape(2, 2, 128, 512)

    part_a(2)
    ring_a1.send_far()
    part_b(2)
    ring_b1.send_far()
    qd.send_down_plane()
    for way, i in ((0, 1), (1, 3)):
        part_a(i)
        ring_a1.send_near(way)
        part_b(i)
        ring_b1.send_near(way)
    part_a(0)
    part_b(0)
    for ring in (ring_a1, ring_b1):
        for way in range(2):
            ring.relay(way)
    qd.send_down_group(None)

    def query_grad(h):
        hs = head(h)
        first, second = causal(g, v, k, h)
        qg[top, hs] = (first + nt(g[top, hs], kv.st[h])).astype(BF)
        qg[low, hs] = (second + nt(g[low, hs], kv.st[h])).astype(BF)

    loop(0, 16, query_grad)
    outs = [pltpu.make_async_copy(qg, qg_hbm, out_sem.at[0])]
    outs[0].start()

    ring_a1.wait_results()
    ring_b1.wait_results()
    for i in range(4):
        part = ring_a1.result(i // 2) if i % 2 == 0 else part
        s1a[i] = part[i % 2].astype(BF).reshape(2, 64, 512)
    ring_a2.send_far()
    ring_a2.send_near(0)
    ring_a2.send_near(1)
    for i in range(4):
        part = ring_b1.result(i // 2) if i % 2 == 0 else part
        s1b[i] = part[i % 2].astype(BF).reshape(2, 64, 512)
    ring_b2.send_far()
    ring_b2.send_near(0)
    ring_b2.send_near(1)

    qd.finish()

    def key_value(h):
        hs = head(h)
        first, second = anti(v, g, q, h)
        kg[top, hs] = (first + nt(v[top, hs], qd.st[h])).astype(BF)
        kg[low, hs] = (second + nt(v[low, hs], qd.st[h])).astype(BF)
        first, second = anti(k, q, g, h)
        vg[top, hs] = (first + nn(k[top, hs], qd.st[h])).astype(BF)
        vg[low, hs] = (second + nn(k[low, hs], qd.st[h])).astype(BF)

    loop(0, 4, key_value)
    for ring in (ring_a2, ring_b2):
        for way in range(2):
            ring.relay(way)
    loop(4, 8, key_value)
    ring_a2.wait_results()
    ring_b2.wait_results()
    for i, ring in enumerate((ring_a2, ring_b2)):
        for half in range(2):
            part = ring.result(half).astype(BF)
            for j in range(2):
                fin[half * 2 + j, :, pl.ds(512 * i, 512)] = part[32 * j : 32 * j + 32]

    def last(i):
        r = (at.p + i) % 4
        return remote(fin.at[r], fin_land.at[at.p], fin_sem.at[0, i - 1], fin_sem.at[1, i - 1], at.group(r))

    for i in range(1, 4):
        last(i).start()
    fin_land[at.p] = fin[at.p]
    loop(8, 16, key_value)
    outs.append(pltpu.make_async_copy(kg, kg_hbm, out_sem.at[1]))
    outs[1].start()
    outs.append(pltpu.make_async_copy(vg, vg_hbm, out_sem.at[2]))
    outs[2].start()
    for i in range(1, 4):
        last(i).wait()
    for d in range(2):
        wg[:, pl.ds(1024 * d, 1024)] = fin_land[d].astype(F32) + fin_land[2 + d].astype(F32)
    outs.append(pltpu.make_async_copy(wg, wg_hbm, out_sem.at[3]))
    outs[3].start()
    for out in outs:
        out.wait()


def scan_scratch():
    return (
        VM((16, 128, 128), BF),
        VM((4, 4, 128, 128), BF),
        VM((16, 32, 128), F32),
        VM((16, 32, 128), F32),
        VM((16, 32, 128), F32),
        VM((16, 32, 128), F32),
        VM((4, 4, 128, 128), BF),
        VM((16, 128, 128), BF),
        DMA((2, 3)),
        DMA((2, 3)),
        DMA((2,)),
        DMA((2,)),
    )


def local(queries, keys, values, cotangent, out_weight, memory):
    tok = VM((512, 2048), BF)
    any_spec = pl.BlockSpec(memory_space=pl.ANY)
    like = jax.ShapeDtypeStruct((512, 2048), BF)
    return pl.pallas_call(
        kernel,
        out_shape=(like, like, like, jax.ShapeDtypeStruct((32, 2048), F32)),
        in_specs=[any_spec] * 6,
        out_specs=(any_spec,) * 4,
        scratch_shapes=[
            tok, tok, tok,
            VM((2, 2048, 1024), BF),
            VM((2, 512, 1024), BF),
            VM((512, 1024), BF),
            VM((4, 128, 128), F32),
            VM((512, 2048), F32),
            tok,
            VM((16, 512, 128), F32),
            scan_scratch(),
            scan_scratch(),
            VM((2, 4, 4, 128, 512), BF),
            VM((4, 2, 2, 128, 512), BF),
            VM((4, 2, 2, 128, 512), BF),
            VM((2, 3, 2, 128, 512), BF),
            VM((2, 3, 2, 128, 512), BF),
            VM((4, 2, 64, 512), BF),
            VM((4, 2, 64, 512), BF),
            VM((2, 3, 64, 512), BF),
            VM((2, 3, 64, 512), BF),
            VM((4, 32, 1024), BF),
            VM((4, 32, 1024), BF),
            tok, tok, tok,
            VM((32, 2048), F32),
            DMA((7,)),
            DMA((4,)),
            DMA((2,)),
            DMA((2,)),
            DMA((2, 4)),
            DMA((4, 2, 2, 3)),
            DMA((2, 3)),
        ],
        compiler_params=pltpu.CompilerParams(
            collective_id=0, has_side_effects=True, vmem_limit_bytes=67043328
        ),
    )(queries, keys, values, cotangent, out_weight, memory)


def solution(mesh):
    in_specs = (
        P("ctx", "tp"),
        P("ctx", "tp"),
        P("ctx", "tp"),
        P("ctx", "tp"),
        P("tp", None),
        P("tp", None, None),
    )
    out_specs = (P("ctx", "tp"), P("ctx", "tp"), P("ctx", "tp"), P(("tp", "ctx"), None))
    return jax.shard_map(local, mesh=mesh, in_specs=in_specs, out_specs=out_specs, check_vma=False)
```

time: 1110 us -> 117 us (0.11)
  waiting for transfers between devices: 772 us -> 0 us
  other arithmetic: 207 us -> 0 us
  Pallas kernels: 0 us -> 108 us
  matrix products: 81.7 us -> 0 us
  local copies, waits for them, and re-layouts: 22.7 us -> 7.68 us
  between operations: 13.9 us -> 0.65 us
    all_gather x3 -> x0, waiting for transfers between devices: 584 us -> none  [the longest x2 550 us: carried_in(): everything = lax.all_gather(value, axis)]
    select_n x128 -> x0, other arithmetic: 205 us -> none  [lap(): return jnp.where(reached, new, before)]
    reduce_scatter x1 -> x0, waiting for transfers between devices: 187 us -> none  [local(): lax.psum_scatter(lax.dot_general(attended, full_cot, (((0,), (0,)), ((),...]
    pallas_call x0 -> x1, Pallas kernels: none -> 108 us  [local(): pl.pallas_call(kernel, out_shape=(like, like, like, jax.ShapeDtypeStruct(...]
    dot_general x14 -> x0, matrix products: 81.7 us -> none  [the longest x1 12.7 us: local(): lax.dot_general(attended, full_cot, (((0,), (0,)), ((), ())), preferred_e...]
  transfers between devices with their start and end apart: 4 -> 0, of which waited for: 4 -> 0; matrix products, arithmetic and copies ran while one was open for 28% -> 0% of each run, Pallas kernels for 0% -> 0%
where the time goes in v1:
time: 117 us
  Pallas kernels  108 us (92%)
  local copies, waits for them, and re-layouts  7.68 us (7%)
    pallas_call x1, Pallas kernels, local(): pl.pallas_call(kernel, out_shape=(like, like, like, jax.ShapeDtypeStruct(...  108 us
    unnamed x10, local copies, waits for them, and re-layouts  7.68 us

profile of v1, /device:TPU:1, one launch (start us, length us, event | category | flops | bytes accessed | tf_op | source)
XLA Modules:
  0.0 116.8 jit_solution(3138938817081092770)
XLA Ops:
  0.6 108.5 %shard_map.93 = (bf16[512,2048]{1,0:T(8,128)(2,1)}, bf16[512,2048]{1,0:T(8,128)(2,1)}, bf16[512,2048]{1,0:T(8,128)(2,1)}, f32[32,2048]{1,0:T(8,128)}) custom-call(bf16[512,2048]{1,0:T(8,128)(2,1)} %q_hbm.1, bf16[512,2048]{1,0:T(8,128)(2,1)} %k_hbm.1, bf16[512,2048]{1,0:T(8,128)(2,1)} %v_hbm.1, bf16[512,1024]{1,0:T(8,128)(2,1)} %cot_hbm.1, ...), custom_call_target="tpu_custom_call" | custom-call | tf_op jit(solution)/shard_map/pallas_call | solution.py:451
  109.1 0.0 copy-start.1
  109.1 3.3 %copy.14 = bf16[512,2048]{1,0:T(8,128)(2,1)} copy(bf16[512,2048]{1,0:T(8,128)(2,1)} %get-tuple-element.8) | data formatting | bytes 4194304
  112.4 0.0 copy-done.1
  112.4 0.0 copy-start
  112.4 1.3 %copy.15 = bf16[512,2048]{1,0:T(8,128)(2,1)} copy(bf16[512,2048]{1,0:T(8,128)(2,1)S(1)} %copy-done.1) | data formatting | bytes 4194304
  113.7 1.0 copy-done
  114.8 0.0 copy-start.2
  114.8 1.3 %copy.16 = bf16[512,2048]{1,0:T(8,128)(2,1)} copy(bf16[512,2048]{1,0:T(8,128)(2,1)S(1)} %copy-done) | data formatting | bytes 4194304
  116.1 0.0 copy-done.2
  116.1 0.7 copy.17
Async XLA Ops:
  109.1 3.3 %copy-start.1 = (bf16[512,2048]{1,0:T(8,128)(2,1)S(1)}, bf16[512,2048]{1,0:T(8,128)(2,1)}, u32[]{:S(2)}) copy-start(bf16[512,2048]{1,0:T(8,128)(2,1)} %get-tuple-element.9) | copy-start | bytes 6291460
  112.4 2.3 %copy-start = (bf16[512,2048]{1,0:T(8,128)(2,1)S(1)}, bf16[512,2048]{1,0:T(8,128)(2,1)}, u32[]{:S(2)}) copy-start(bf16[512,2048]{1,0:T(8,128)(2,1)} %get-tuple-element.10) | copy-start | bytes 6291460
  114.8 1.3 %copy-start.2 = (f32[32,2048]{1,0:T(8,128)S(1)}, f32[32,2048]{1,0:T(8,128)}, u32[]{:S(2)}) copy-start(f32[32,2048]{1,0:T(8,128)} %get-tuple-element.11) | copy-start | bytes 786436

commit v2 on v1

v2 whole, which is shorter than its diff:
```python
import jax
import jax.numpy as jnp
from jax import lax
from jax.experimental import pallas as pl
from jax.experimental.pallas import tpu as pltpu
from jax.sharding import PartitionSpec as P

MESH = pl.DeviceIdType.MESH
BF = jnp.bfloat16
F32 = jnp.float32
VM = pltpu.VMEM
DMA = pltpu.SemaphoreType.DMA


def nn(a, b):
    return lax.dot_general(a, b, (((1,), (0,)), ((), ())), preferred_element_type=F32)


def nt(a, b):
    return lax.dot_general(a, b, (((1,), (1,)), ((), ())), preferred_element_type=F32)


def tn(a, b):
    return lax.dot_general(a, b, (((0,), (0,)), ((), ())), preferred_element_type=F32)


def head(h):
    return pl.ds(pl.multiple_of(h * 128, 128), 128)


def loop(lo, hi, body):
    side = 4 if (hi - lo) % 4 == 0 else 2

    def step(i, carry):
        for j in range(side):
            body(lo + side * i + j)
        return carry

    lax.fori_loop(0, (hi - lo) // side, step, 0)


def each(lo, hi, body):
    def step(i, carry):
        body(i)
        return carry

    lax.fori_loop(lo, hi, step, 0)


class Place:
    def __init__(self):
        self.me = lax.axis_index("ctx")
        self.tp = lax.axis_index("tp")
        self.p = self.me % 4
        self.core = self.me % 2
        self.x = self.p // 2
        self.zy = self.me // 4
        self.z = self.me // 16
        self.y = self.zy % 4
        self.base = self.me - self.p

    def other_core(self):
        return (self.base + 2 * self.x + 1 - self.core, self.tp)

    def other_x(self):
        return (self.base + 2 * (1 - self.x) + self.core, self.tp)

    def group(self, p):
        return (self.base + p, self.tp)

    def plane(self, zy):
        return (zy * 4 + self.p, self.tp)

    def along_y(self, y):
        return (self.me + (y - self.y) * 4, self.tp)

    def along_z(self, z):
        return (self.me + (z - self.z) * 16, self.tp)


def remote(src, dst, send, recv, device):
    return pltpu.make_async_remote_copy(
        src_ref=src, dst_ref=dst, send_sem=send, recv_sem=recv, device_id=device, device_id_type=MESH
    )


class Scan:
    def __init__(self, at, refs, reverse):
        self.at, self.reverse = at, reverse
        (self.s, self.a, self.pc, self.px, self.t, self.b, self.pre, self.c, self.e, self.f, self.d, self.st,
         self.sem, self.up, self.down) = refs
        self.copies = [
            remote(self.s.at[pl.ds(8 * (1 - at.core), 8)], self.a, self.sem.at[0, 0], self.sem.at[1, 0], at.other_core()),
            remote(self.pc.at[1 - at.x], self.px, self.sem.at[0, 1], self.sem.at[1, 1], at.other_x()),
            remote(self.e, self.f, self.sem.at[0, 2], self.sem.at[1, 2], at.other_x()),
            remote(self.d, self.st.at[pl.ds(8 * at.core, 8)], self.sem.at[0, 3], self.sem.at[1, 3], at.other_core()),
        ]

    def send_core(self):
        self.copies[0].start()

    def send_x(self):
        self.copies[0].wait()
        for i in range(2):
            for h in range(4):
                own = self.s[8 * self.at.core + 4 * i + h].astype(F32)
                self.pc[i, h] = (own + self.a[4 * i + h].astype(F32)).astype(BF)
        self.copies[1].start()

    def up_plane(self, k):
        j = (self.at.zy + k) % 16
        return remote(self.t.at[j], self.b.at[self.at.zy], self.up.at[0], self.up.at[1], self.at.plane(j))

    def send_up(self):
        self.copies[1].wait()
        for h in range(4):
            total = self.pc[self.at.x, h].astype(F32) + self.px[h].astype(F32)
            self.t[pl.ds(4 * h, 4)] = total.reshape(4, 32, 128)
        each(1, 16, lambda k: self.up_plane(k).start())
        self.b[self.at.zy] = self.t[self.at.zy]

    def down_plane(self, k):
        j = (self.at.zy + k) % 16
        return remote(self.pre.at[j], self.c.at[self.at.zy], self.down.at[0], self.down.at[1], self.at.plane(j))

    def wait_all(self, src, dst, sems):
        pltpu.make_async_copy(src.at[pl.ds(0, 15)], src.at[pl.ds(0, 15)], sems.at[0]).wait()
        pltpu.make_async_copy(dst.at[pl.ds(0, 15)], dst.at[pl.ds(0, 15)], sems.at[1]).wait()

    def send_down(self):
        self.wait_all(self.t, self.b, self.up)
        run = jnp.zeros((32, 128), F32)
        for i in reversed(range(16)) if self.reverse else range(16):
            self.pre[i] = run
            run = run + self.b[i]
        each(1, 16, lambda k: self.down_plane(k).start())
        self.c[self.at.zy] = self.pre[self.at.zy]

    def send_back_x(self, memory):
        self.wait_all(self.pre, self.c, self.down)
        after = self.at.x == (0 if self.reverse else 1)
        for h in range(4):
            run = self.c[pl.ds(4 * h, 4)].reshape(128, 128)
            if memory is not None:
                run = run + memory[h]
            mine, theirs = self.pc[self.at.x, h].astype(F32), self.px[h].astype(F32)
            self.e[h] = (run + jnp.where(after, 0.0, mine)).astype(BF)
            self.c[pl.ds(4 * h, 4)] = (run + jnp.where(after, theirs, 0.0)).reshape(4, 32, 128)
        self.copies[2].start()

    def send_back_core(self):
        self.copies[2].wait()
        after = self.at.core == (0 if self.reverse else 1)
        first = 8 * self.at.core

        def settle(run, h):
            mine, theirs = self.s[first + h].astype(F32), self.a[h].astype(F32)
            self.d[h] = (run + jnp.where(after, 0.0, mine)).astype(BF)
            self.st[first + h] = (run + jnp.where(after, theirs, 0.0)).astype(BF)

        for h in range(4):
            settle(self.c[pl.ds(4 * h, 4)].reshape(128, 128), 4 * self.at.x + h)
            settle(self.f[h].astype(F32), 4 * (1 - self.at.x) + h)
        self.copies[3].start()

    def finish(self):
        self.copies[3].wait()


class Ring:
    def __init__(self, src, land, sems, pos, device):
        self.src, self.land, self.sems, self.pos = src, land, sems, pos
        self.quarters = [pos, (pos + 1) % 4, (pos + 2) % 4, (pos + 3) % 4]
        self.device = device

    def copy(self, way, slot):
        near = self.quarters[1] if way == 0 else self.quarters[3]
        if slot == 0:
            src = self.src.at[self.quarters[2], way]
        elif slot == 1:
            src = self.src.at[near, 1 - way]
        else:
            src = self.src.at[near, way]
        return remote(
            src, self.land.at[way, slot], self.sems.at[0, way, slot], self.sems.at[1, way, slot], self.device(near)
        )

    def send_far(self):
        self.copy(0, 0).start()
        self.copy(1, 0).start()

    def send_near(self, way):
        self.copy(way, 1).start()

    def relay(self, way):
        near = self.quarters[1] if way == 0 else self.quarters[3]
        self.copy(way, 0).wait()
        self.src[near, way] = (self.src[near, way].astype(F32) + self.land[way, 0].astype(F32)).astype(BF)
        self.copy(way, 2).start()

    def result(self, half):
        own = self.src[self.pos, half].astype(F32)
        for way in range(2):
            slot = 2 if way == half else 1
            own = own + self.land[way, slot].astype(F32)
        return own

    def wait_results(self):
        for way in range(2):
            self.copy(way, 1).wait()
            self.copy(way, 2).wait()


def kernel(
    q_hbm, k_hbm, v_hbm, cot_hbm, w_hbm, mem_hbm,
    qg, kg, vg, wg,
    q, k, v, w, cot, pcot, mem, gacc, g, intra,
    kv_refs, qd_refs,
    sup, att, pa, pb, land_a1, land_b1, s1a, s1b, land_a2, land_b2, fin, fin_land,
    in_sem, tp_sem, pc_sem, at_sem, ring_sem, fin_sem,
):
    at = Place()
    me, tp, core = at.me, at.tp, at.core
    peer_core = at.other_core()
    peer_tp = (me, 1 - tp)

    loads = [
        pltpu.make_async_copy(k_hbm, k, in_sem.at[0]),
        pltpu.make_async_copy(v_hbm, v, in_sem.at[1]),
        pltpu.make_async_copy(q_hbm, q, in_sem.at[2]),
        pltpu.make_async_copy(cot_hbm, cot.at[tp], in_sem.at[3]),
        pltpu.make_async_copy(w_hbm.at[:, pl.ds(0, 1024)], w.at[0], in_sem.at[4]),
        pltpu.make_async_copy(w_hbm.at[:, pl.ds(1024, 1024)], w.at[1], in_sem.at[5]),
        pltpu.make_async_copy(mem_hbm.at[pl.ds(8 * core + 4 * at.x, 4)], mem, in_sem.at[6]),
    ]
    for load in loads:
        load.start()

    barrier = pltpu.get_barrier_semaphore()

    def signal(device):
        pl.semaphore_signal(barrier, inc=1, device_id=device, device_id_type=MESH)

    signal(peer_tp)
    for i in range(1, 4):
        signal(at.group((at.p + i) % 4))
    each(1, 16, lambda i: signal(at.plane((at.zy + i) % 16)))

    def mine(c):
        return pl.ds(pl.multiple_of(c * 512, 512), 512)

    cot_copies = [
        remote(cot_hbm.at[rows], cot.at[tp, rows], tp_sem.at[0, i], tp_sem.at[1, i], peer_tp)
        for i, rows in enumerate((pl.ds(0, 64), pl.ds(64, 192), pl.ds(256, 128), pl.ds(384, 128)))
    ]
    near_cot = remote(cot_hbm.at[:, mine(1 - core)], pcot.at[0], pc_sem.at[0, 0], pc_sem.at[1, 0], peer_core)
    far_cot = remote(cot.at[1 - tp, :, mine(1 - core)], pcot.at[1], pc_sem.at[0, 1], pc_sem.at[1, 1], peer_core)

    kv = Scan(at, kv_refs, False)
    qd = Scan(at, qd_refs, True)

    loads[0].wait()
    loads[1].wait()

    def kv_sum(h):
        kv.s[h] = tn(k[:, head(h)], v[:, head(h)]).astype(BF)

    loop(0, 16, kv_sum)
    pl.semaphore_wait(barrier, 19)
    kv.send_core()
    cot_copies[0].start()
    near_cot.start()

    loads[2].wait()
    row = lax.broadcasted_iota(jnp.int32, (256, 256), 0)
    col = lax.broadcasted_iota(jnp.int32, (256, 256), 1)

    def lower(x):
        return jnp.where(row >= col, x, 0.0).astype(BF)

    def upper(x):
        return jnp.where(row <= col, x, 0.0).astype(BF)

    top, low = pl.ds(0, 256), pl.ds(256, 256)

    def causal(a, b, c, h):
        hs = head(h)
        a0, a1, b0, b1, c0, c1 = a[top, hs], a[low, hs], b[top, hs], b[low, hs], c[top, hs], c[low, hs]
        first = nn(lower(nt(a0, b0)), c0)
        second = nn(nt(a1, b0).astype(BF), c0) + nn(lower(nt(a1, b1)), c1)
        return first, second

    def anti(b, a, c, h):
        hs = head(h)
        a0, a1, b0, b1, c0, c1 = a[top, hs], a[low, hs], b[top, hs], b[low, hs], c[top, hs], c[low, hs]
        first = nn(upper(nt(b0, a0)), c0) + nn(nt(b0, a1).astype(BF), c1)
        second = nn(upper(nt(b1, a1)), c1)
        return first, second

    def scored(h):
        first, second = causal(q, k, v, h)
        intra[h, top] = first
        intra[h, low] = second

    def turned(h):
        hs = head(h)
        k0, k1, q0, q1 = k[top, hs], k[low, hs], q[top, hs], q[low, hs]
        sup[h, 0] = upper(nt(k0, q0))
        sup[h, 1] = nt(k0, q1).astype(BF)
        sup[h, 2] = upper(nt(k1, q1))

    loop(0, 4, scored)
    kv.send_x()
    cot_copies[1].start()
    cot_copies[2].start()
    loop(4, 16, scored)
    kv.send_up()

    for load in loads[3:6]:
        load.wait()

    def wrows(n):
        return pl.ds(pl.multiple_of(n * 256, 256), 256)

    def grad_own(n):
        gacc[:, wrows(n)] = nt(cot[tp], w[tp, wrows(n), :])

    each(0, 8, grad_own)
    loop(0, 8, turned)
    kv.send_down()

    def grad_top(n):
        g[top, wrows(n)] = (gacc[top, wrows(n)] + nt(cot[1 - tp, top, :], w[1 - tp, wrows(n), :])).astype(BF)

    def grad_low(n):
        g[low, wrows(n)] = (gacc[low, wrows(n)] + nt(cot[1 - tp, low, :], w[1 - tp, wrows(n), :])).astype(BF)

    loads[6].wait()
    cot_copies[0].wait()
    cot_copies[1].wait()
    each(0, 8, grad_top)
    kv.send_back_x(mem)
    cot_copies[3].start()
    loop(8, 16, turned)
    kv.send_back_core()
    kv.finish()

    def attend(h):
        a = intra[h] + nn(q[:, head(h)], kv.st[h])
        att[0, h // 4, h % 4] = a.T.astype(BF)

    att_copies = []
    for i in range(4):
        loop(4 * i, 4 * i + 4, attend)
        att_copies.append(remote(att.at[0, i], att.at[1, i], at_sem.at[0, i], at_sem.at[1, i], peer_core))
        att_copies[i].start()

    def query_top(h):
        hs = head(h)
        g0 = g[top, hs]
        qg[top, hs] = (nn(lower(nt(g0, v[top, hs])), k[top, hs]) + nt(g0, kv.st[h])).astype(BF)

    def query_low(h):
        hs = head(h)
        g1 = g[low, hs]
        r = nn(nt(g1, v[top, hs]).astype(BF), k[top, hs]) + nn(lower(nt(g1, v[low, hs])), k[low, hs])
        qg[low, hs] = (r + nt(g1, kv.st[h])).astype(BF)

    loop(0, 16, query_top)
    near_cot.wait()
    for copy in att_copies:
        copy.wait()

    y, z = at.y, at.z
    ring_a1 = Ring(pa, land_a1, ring_sem.at[0], y, at.along_y)
    ring_b1 = Ring(pb, land_b1, ring_sem.at[1], z, at.along_z)
    ring_a2 = Ring(s1a, land_a2, ring_sem.at[2], z, at.along_z)
    ring_b2 = Ring(s1b, land_b2, ring_sem.at[3], y, at.along_y)

    def part_a(i):
        yq = ring_a1.quarters[i]
        r = nn(att[0, :, yq].reshape(512, 512), cot[tp, :, mine(core)])
        r = r + nn(att[1, :, yq].reshape(512, 512), pcot[0])
        pa[yq] = r.astype(BF).reshape(2, 2, 128, 512)

    def part_b(i):
        zq = ring_b1.quarters[i]
        r = nn(att[0, zq].reshape(512, 512), cot[1 - tp, :, mine(core)])
        r = r + nn(att[1, zq].reshape(512, 512), pcot[1])
        pb[zq] = r.astype(BF).reshape(2, 2, 128, 512)

    part_a(2)
    ring_a1.send_far()
    cot_copies[2].wait()
    cot_copies[3].wait()
    far_cot.start()
    each(0, 8, grad_low)

    def qd_sum(h):
        qd.s[h] = tn(q[:, head(h)], g[:, head(h)]).astype(BF)

    loop(0, 16, qd_sum)
    qd.send_core()
    far_cot.wait()
    part_b(2)
    ring_b1.send_far()
    part_a(1)
    ring_a1.send_near(0)
    qd.send_x()
    part_a(3)
    ring_a1.send_near(1)
    part_b(1)
    ring_b1.send_near(0)
    part_b(3)
    ring_b1.send_near(1)
    loop(0, 4, query_low)
    qd.send_up()
    ring_a1.relay(0)
    ring_a1.relay(1)
    part_a(0)
    part_b(0)

    def key_scored(h):
        first, second = anti(v, g, q, h)
        intra[h, top] = first
        intra[h, low] = second

    def value_scored(h):
        g0, g1 = g[top, head(h)], g[low, head(h)]
        gacc[top, head(h)] = nn(sup[h, 0], g0) + nn(sup[h, 1], g1)
        gacc[low, head(h)] = nn(sup[h, 2], g1)

    loop(4, 8, query_low)
    ring_b1.relay(0)
    ring_b1.relay(1)
    loop(8, 16, query_low)
    loop(0, 4, key_scored)
    qd.send_down()

    def stage_two(first, second, to):
        first.wait_results()
        for half in range(2):
            part = first.result(half)
            for i in range(2):
                to[2 * half + i] = part[i].astype(BF).reshape(2, 64, 512)
        second.send_far()
        second.send_near(0)
        second.send_near(1)

    loop(4, 8, key_scored)
    stage_two(ring_a1, ring_a2, s1a)
    loop(8, 12, key_scored)
    stage_two(ring_b1, ring_b2, s1b)
    loop(12, 16, key_scored)
    qd.send_back_x(None)
    ring_a2.relay(0)
    ring_a2.relay(1)
    loop(0, 4, value_scored)
    ring_b2.relay(0)
    ring_b2.relay(1)
    loop(4, 12, value_scored)
    qd.send_back_core()
    loop(12, 16, value_scored)
    ring_a2.wait_results()
    ring_b2.wait_results()
    for i, ring in enumerate((ring_a2, ring_b2)):
        for half in range(2):
            part = ring.result(half).astype(BF)
            for j in range(2):
                fin[half * 2 + j, :, pl.ds(512 * i, 512)] = part[32 * j : 32 * j + 32]

    def last(i):
        r = (at.p + i) % 4
        return remote(fin.at[r], fin_land.at[at.p], fin_sem.at[0, i - 1], fin_sem.at[1, i - 1], at.group(r))

    for i in range(1, 4):
        last(i).start()
    fin_land[at.p] = fin[at.p]
    qd.finish()

    def key_grad(h):
        hs = head(h)
        kg[:, hs] = (intra[h] + nt(v[:, hs], qd.st[h])).astype(BF)

    def value_grad(h):
        hs = head(h)
        vg[:, hs] = (gacc[:, hs] + nn(k[:, hs], qd.st[h])).astype(BF)

    loop(0, 16, key_grad)
    loop(0, 16, value_grad)
    for i in range(1, 4):
        last(i).wait()
    for c in range(2):
        r = fin_land[c].astype(F32) + fin_land[2 + c].astype(F32)
        wg[:, pl.ds(pl.multiple_of(tp * 1024 + c * 512, 512), 512)] = r[:, :512]
        wg[:, pl.ds(pl.multiple_of((1 - tp) * 1024 + c * 512, 512), 512)] = r[:, 512:]


def scan_scratch():
    piece = VM((16, 32, 128), F32)
    return (
        VM((16, 128, 128), BF),
        VM((8, 128, 128), BF),
        VM((2, 4, 128, 128), BF),
        VM((4, 128, 128), BF),
        piece, piece, piece, piece,
        VM((4, 128, 128), BF),
        VM((4, 128, 128), BF),
        VM((8, 128, 128), BF),
        VM((16, 128, 128), BF),
        DMA((2, 4)),
        DMA((2,)),
        DMA((2,)),
    )


def local(queries, keys, values, cotangent, out_weight, memory):
    tok = VM((512, 2048), BF)
    any_spec = pl.BlockSpec(memory_space=pl.ANY)
    like = jax.ShapeDtypeStruct((512, 2048), BF)
    return pl.pallas_call(
        kernel,
        out_shape=(VM((512, 2048), BF), VM((512, 2048), BF), VM((512, 2048), BF), VM((32, 2048), F32)),
        in_specs=[any_spec] * 6,
        out_specs=(pl.BlockSpec(memory_space=VM),) * 4,
        scratch_shapes=[
            tok, tok, tok,
            VM((2, 2048, 1024), BF),
            VM((2, 512, 1024), BF),
            VM((2, 512, 512), BF),
            VM((4, 128, 128), F32),
            VM((512, 2048), F32),
            tok,
            VM((16, 512, 128), F32),
            scan_scratch(),
            scan_scratch(),
            VM((16, 3, 256, 256), BF),
            VM((2, 4, 4, 128, 512), BF),
            VM((4, 2, 2, 128, 512), BF),
            VM((4, 2, 2, 128, 512), BF),
            VM((2, 3, 2, 128, 512), BF),
            VM((2, 3, 2, 128, 512), BF),
            VM((4, 2, 64, 512), BF),
            VM((4, 2, 64, 512), BF),
            VM((2, 3, 64, 512), BF),
            VM((2, 3, 64, 512), BF),
            VM((4, 32, 1024), BF),
            VM((4, 32, 1024), BF),
            DMA((7,)),
            DMA((2, 4)),
            DMA((2, 2)),
            DMA((2, 4)),
            DMA((4, 2, 2, 3)),
            DMA((2, 3)),
        ],
        compiler_params=pltpu.CompilerParams(
            collective_id=0, has_side_effects=True, vmem_limit_bytes=59768832
        ),
    )(queries, keys, values, cotangent, out_weight, memory)


def solution(mesh):
    in_specs = (
        P("ctx", "tp"),
        P("ctx", "tp"),
        P("ctx", "tp"),
        P("ctx", "tp"),
        P("tp", None),
        P("tp", None, None),
    )
    out_specs = (P("ctx", "tp"), P("ctx", "tp"), P("ctx", "tp"), P(("tp", "ctx"), None))
    return jax.shard_map(local, mesh=mesh, in_specs=in_specs, out_specs=out_specs, check_vma=False)
```

time: 117 us -> 90.6 us (0.77)
  Pallas kernels: 108 us -> 85.1 us
  local copies, waits for them, and re-layouts: 7.68 us -> 4.66 us
    pallas_call x1, Pallas kernels: 108 us -> 85.1 us  [local(): pl.pallas_call(kernel, out_shape=(VM((512, 2048), BF), VM((512, 2048), BF...]
    unnamed x10 -> x4, local copies, waits for them, and re-layouts: 7.68 us -> 4.66 us
where the time goes in v2:
time: 90.6 us; the launch traced here: 90.4 us
  Pallas kernels  85.1 us (94%)
  local copies, waits for them, and re-layouts  4.66 us (5%)
    pallas_call x1, Pallas kernels, local(): pl.pallas_call(kernel, out_shape=(VM((512, 2048), BF), VM((512, 2048), BF...  85.1 us
    unnamed x4, local copies, waits for them, and re-layouts  4.66 us

profile of v2, /device:TPU:1, one launch (start us, length us, event | category | flops | bytes accessed | tf_op | source)
XLA Modules:
  0.0 90.4 jit_solution(4100323280047318555)
XLA Ops:
  0.6 85.1 %shard_map.93 = (bf16[512,2048]{1,0:T(8,128)(2,1)S(1)}, bf16[512,2048]{1,0:T(8,128)(2,1)S(1)}, bf16[512,2048]{1,0:T(8,128)(2,1)S(1)}, f32[32,2048]{1,0:T(8,128)S(1)}) custom-call(bf16[512,2048]{1,0:T(8,128)(2,1)} %q_hbm.1, bf16[512,2048]{1,0:T(8,128)(2,1)} %k_hbm.1, bf16[512,2048]{1,0:T(8,128)(2,1)} %v_hbm.1, bf16[512,1024]{1,0:T(8,128)(2,1)} %cot_hbm.1, ...), custom_call_target="tpu_custom_call" | custom-call | tf_op jit(solution)/shard_map/pallas_call | solution.py:521
  85.8 1.3 %copy.14 = bf16[512,2048]{1,0:T(8,128)(2,1)} copy(bf16[512,2048]{1,0:T(8,128)(2,1)S(1)} %get-tuple-element.4) | data formatting | bytes 4194304
  87.1 0.7 copy.17
  87.8 1.3 %copy.15 = bf16[512,2048]{1,0:T(8,128)(2,1)} copy(bf16[512,2048]{1,0:T(8,128)(2,1)S(1)} %get-tuple-element.5) | data formatting | bytes 4194304
  89.1 1.3 %copy.16 = bf16[512,2048]{1,0:T(8,128)(2,1)} copy(bf16[512,2048]{1,0:T(8,128)(2,1)S(1)} %get-tuple-element.6) | data formatting | bytes 4194304

commit v3 on v2

--- a/solution.py
+++ b/solution.py
@@ -87,7 +87,7 @@
 class Scan:
     def __init__(self, at, refs, reverse):
         self.at, self.reverse = at, reverse
-        (self.s, self.a, self.pc, self.px, self.t, self.b, self.pre, self.c, self.e, self.f, self.d, self.st,
+        (self.s, self.a, self.pc, self.px, self.t, self.b, self.pre, self.c, self.run, self.e, self.f, self.d, self.st,
          self.sem, self.up, self.down) = refs
         self.copies = [
             remote(self.s.at[pl.ds(8 * (1 - at.core), 8)], self.a, self.sem.at[0, 0], self.sem.at[1, 0], at.other_core()),
@@ -115,7 +115,7 @@
         self.copies[1].wait()
         for h in range(4):
             total = self.pc[self.at.x, h].astype(F32) + self.px[h].astype(F32)
-            self.t[pl.ds(4 * h, 4)] = total.reshape(4, 32, 128)
+            self.t[pl.ds(4 * h, 4)] = total.reshape(4, 32, 128).astype(self.t.dtype)
         each(1, 16, lambda k: self.up_plane(k).start())
         self.b[self.at.zy] = self.t[self.at.zy]
 
@@ -131,8 +131,8 @@
         self.wait_all(self.t, self.b, self.up)
         run = jnp.zeros((32, 128), F32)
         for i in reversed(range(16)) if self.reverse else range(16):
-            self.pre[i] = run
-            run = run + self.b[i]
+            self.pre[i] = run.astype(self.pre.dtype)
+            run = run + self.b[i].astype(F32)
         each(1, 16, lambda k: self.down_plane(k).start())
         self.c[self.at.zy] = self.pre[self.at.zy]
 
@@ -140,12 +140,12 @@
         self.wait_all(self.pre, self.c, self.down)
         after = self.at.x == (0 if self.reverse else 1)
         for h in range(4):
-            run = self.c[pl.ds(4 * h, 4)].reshape(128, 128)
+            run = self.c[pl.ds(4 * h, 4)].astype(F32).reshape(128, 128)
             if memory is not None:
                 run = run + memory[h]
             mine, theirs = self.pc[self.at.x, h].astype(F32), self.px[h].astype(F32)
             self.e[h] = (run + jnp.where(after, 0.0, mine)).astype(BF)
-            self.c[pl.ds(4 * h, 4)] = (run + jnp.where(after, theirs, 0.0)).reshape(4, 32, 128)
+            self.run[h] = run + jnp.where(after, theirs, 0.0)
         self.copies[2].start()
 
     def send_back_core(self):
@@ -159,7 +159,7 @@
             self.st[first + h] = (run + jnp.where(after, theirs, 0.0)).astype(BF)
 
         for h in range(4):
-            settle(self.c[pl.ds(4 * h, 4)].reshape(128, 128), 4 * self.at.x + h)
+            settle(self.run[h], 4 * self.at.x + h)
             settle(self.f[h].astype(F32), 4 * (1 - self.at.x) + h)
         self.copies[3].start()
 
@@ -216,7 +216,7 @@
     qg, kg, vg, wg,
     q, k, v, w, cot, pcot, mem, gacc, g, intra,
     kv_refs, qd_refs,
-    sup, att, pa, pb, land_a1, land_b1, s1a, s1b, land_a2, land_b2, fin, fin_land,
+    sup, qacc, att, parts, lands, s1a, s1b, land_a2, land_b2, fin, fin_land,
     in_sem, tp_sem, pc_sem, at_sem, ring_sem, fin_sem,
 ):
     at = Place()
@@ -225,14 +225,19 @@
     peer_tp = (me, 1 - tp)
 
     loads = [
-        pltpu.make_async_copy(k_hbm, k, in_sem.at[0]),
-        pltpu.make_async_copy(v_hbm, v, in_sem.at[1]),
         pltpu.make_async_copy(q_hbm, q, in_sem.at[2]),
         pltpu.make_async_copy(cot_hbm, cot.at[tp], in_sem.at[3]),
         pltpu.make_async_copy(w_hbm.at[:, pl.ds(0, 1024)], w.at[0], in_sem.at[4]),
         pltpu.make_async_copy(w_hbm.at[:, pl.ds(1024, 1024)], w.at[1], in_sem.at[5]),
         pltpu.make_async_copy(mem_hbm.at[pl.ds(8 * core + 4 * at.x, 4)], mem, in_sem.at[6]),
     ]
+    def block(src, dst, i, sem):
+        return pltpu.make_async_copy(src.at[:, pl.ds(512 * i, 512)], dst.at[:, pl.ds(512 * i, 512)], in_sem.at[sem])
+
+    block_loads = [(block(k_hbm, k, i, 7 + i), block(v_hbm, v, i, 11 + i)) for i in range(4)]
+    for pair in block_loads:
+        pair[0].start()
+        pair[1].start()
     for load in loads:
         load.start()
 
@@ -251,7 +256,7 @@
 
     cot_copies = [
         remote(cot_hbm.at[rows], cot.at[tp, rows], tp_sem.at[0, i], tp_sem.at[1, i], peer_tp)
-        for i, rows in enumerate((pl.ds(0, 64), pl.ds(64, 192), pl.ds(256, 128), pl.ds(384, 128)))
+        for i, rows in enumerate((pl.ds(0, 64), pl.ds(64, 192), pl.ds(256, 64), pl.ds(320, 192)))
     ]
     near_cot = remote(cot_hbm.at[:, mine(1 - core)], pcot.at[0], pc_sem.at[0, 0], pc_sem.at[1, 0], peer_core)
     far_cot = remote(cot.at[1 - tp, :, mine(1 - core)], pcot.at[1], pc_sem.at[0, 1], pc_sem.at[1, 1], peer_core)
@@ -259,19 +264,20 @@
     kv = Scan(at, kv_refs, False)
     qd = Scan(at, qd_refs, True)
 
-    loads[0].wait()
-    loads[1].wait()
 
     def kv_sum(h):
         kv.s[h] = tn(k[:, head(h)], v[:, head(h)]).astype(BF)
 
-    loop(0, 16, kv_sum)
+    for i, pair in enumerate(block_loads):
+        pair[0].wait()
+        pair[1].wait()
+        loop(4 * i, 4 * i + 4, kv_sum)
     pl.semaphore_wait(barrier, 19)
     kv.send_core()
     cot_copies[0].start()
     near_cot.start()
 
-    loads[2].wait()
+    loads[0].wait()
     row = lax.broadcasted_iota(jnp.int32, (256, 256), 0)
     col = lax.broadcasted_iota(jnp.int32, (256, 256), 1)
 
@@ -288,13 +294,6 @@
         a0, a1, b0, b1, c0, c1 = a[top, hs], a[low, hs], b[top, hs], b[low, hs], c[top, hs], c[low, hs]
         first = nn(lower(nt(a0, b0)), c0)
         second = nn(nt(a1, b0).astype(BF), c0) + nn(lower(nt(a1, b1)), c1)
-        return first, second
-
-    def anti(b, a, c, h):
-        hs = head(h)
-        a0, a1, b0, b1, c0, c1 = a[top, hs], a[low, hs], b[top, hs], b[low, hs], c[top, hs], c[low, hs]
-        first = nn(upper(nt(b0, a0)), c0) + nn(nt(b0, a1).astype(BF), c1)
-        second = nn(upper(nt(b1, a1)), c1)
         return first, second
 
     def scored(h):
@@ -316,7 +315,7 @@
     loop(4, 16, scored)
     kv.send_up()
 
-    for load in loads[3:6]:
+    for load in loads[1:4]:
         load.wait()
 
     def wrows(n):
@@ -335,13 +334,22 @@
     def grad_low(n):
         g[low, wrows(n)] = (gacc[low, wrows(n)] + nt(cot[1 - tp, low, :], w[1 - tp, wrows(n), :])).astype(BF)
 
-    loads[6].wait()
+    loads[4].wait()
+    loop(8, 16, turned)
     cot_copies[0].wait()
     cot_copies[1].wait()
     each(0, 8, grad_top)
     kv.send_back_x(mem)
     cot_copies[3].start()
-    loop(8, 16, turned)
+
+    def top_rows(h):
+        hs = head(h)
+        g0 = g[top, hs]
+        qacc[h] = tn(q[top, hs], g0)
+        gacc[top, hs] = nn(sup[h, 0], g0)
+        sup[h, 0] = upper(nt(v[top, hs], g0))
+
+    loop(0, 16, top_rows)
     kv.send_back_core()
     kv.finish()
 
@@ -372,138 +380,156 @@
         copy.wait()
 
     y, z = at.y, at.z
-    ring_a1 = Ring(pa, land_a1, ring_sem.at[0], y, at.along_y)
-    ring_b1 = Ring(pb, land_b1, ring_sem.at[1], z, at.along_z)
-    ring_a2 = Ring(s1a, land_a2, ring_sem.at[2], z, at.along_z)
-    ring_b2 = Ring(s1b, land_b2, ring_sem.at[3], y, at.along_y)
-
-    def part_a(i):
-        yq = ring_a1.quarters[i]
-        r = nn(att[0, :, yq].reshape(512, 512), cot[tp, :, mine(core)])
-        r = r + nn(att[1, :, yq].reshape(512, 512), pcot[0])
-        pa[yq] = r.astype(BF).reshape(2, 2, 128, 512)
-
-    def part_b(i):
-        zq = ring_b1.quarters[i]
-        r = nn(att[0, zq].reshape(512, 512), cot[1 - tp, :, mine(core)])
-        r = r + nn(att[1, zq].reshape(512, 512), pcot[1])
-        pb[zq] = r.astype(BF).reshape(2, 2, 128, 512)
-
-    part_a(2)
-    ring_a1.send_far()
+    rings = []
+    for i in range(4):
+        pos, device = (y, at.along_y) if i % 2 == 0 else (z, at.along_z)
+        rings.append(Ring(parts[i], lands[i], ring_sem.at[i], pos, device))
+    ring_y, ring_z = rings[0], rings[1]
+    last_z = Ring(s1a, land_a2, ring_sem.at[4], z, at.along_z)
+    last_y = Ring(s1b, land_b2, ring_sem.at[5], y, at.along_y)
+
+    def part(r, i):
+        n = rings[r].quarters[i]
+        cols = pl.ds(pl.multiple_of(core * 512 + 256 * (r % 2), 256), 256)
+        near = cot[tp, :, cols] if r < 2 else cot[1 - tp, :, cols]
+        far = pcot[r // 2, :, pl.ds(256 * (r % 2), 256)]
+        ours = att[0, :, n] if r % 2 == 0 else att[0, n]
+        theirs = att[1, :, n] if r % 2 == 0 else att[1, n]
+        total = nn(ours.reshape(512, 512), near) + nn(theirs.reshape(512, 512), far)
+        parts[r][n] = total.astype(BF).reshape(2, 2, 128, 256)
+
+    for r in range(2):
+        part(r, 2)
+        rings[r].send_far()
+    for r in range(2):
+        part(r, 1)
+        rings[r].send_near(0)
     cot_copies[2].wait()
     cot_copies[3].wait()
     far_cot.start()
     each(0, 8, grad_low)
 
     def qd_sum(h):
-        qd.s[h] = tn(q[:, head(h)], g[:, head(h)]).astype(BF)
+        qd.s[h] = (qacc[h] + tn(q[low, head(h)], g[low, head(h)])).astype(BF)
 
     loop(0, 16, qd_sum)
     qd.send_core()
+    for r in range(2):
+        part(r, 3)
+        rings[r].send_near(1)
+    qd.send_x()
     far_cot.wait()
-    part_b(2)
-    ring_b1.send_far()
-    part_a(1)
-    ring_a1.send_near(0)
-    qd.send_x()
-    part_a(3)
-    ring_a1.send_near(1)
-    part_b(1)
-    ring_b1.send_near(0)
-    part_b(3)
-    ring_b1.send_near(1)
-    loop(0, 4, query_low)
+    for r in range(2, 4):
+        part(r, 2)
+        rings[r].send_far()
+    for r in range(2):
+        rings[r].relay(0)
+        rings[r].relay(1)
+        part(r, 0)
+    for r in range(2, 4):
+        for i in (1, 3):
+            part(r, i)
     qd.send_up()
-    ring_a1.relay(0)
-    ring_a1.relay(1)
-    part_a(0)
-    part_b(0)
+    for r in range(2, 4):
+        rings[r].send_near(0)
+        rings[r].send_near(1)
+    for r in range(2, 4):
+        part(r, 0)
 
     def key_scored(h):
-        first, second = anti(v, g, q, h)
-        intra[h, top] = first
-        intra[h, low] = second
+        hs = head(h)
+        v0, v1, g1, q1 = v[top, hs], v[low, hs], g[low, hs], q[low, hs]
+        intra[h, top] = nn(sup[h, 0], q[top, hs]) + nn(nt(v0, g1).astype(BF), q1)
+        intra[h, low] = nn(upper(nt(v1, g1)), q1)
 
     def value_scored(h):
-        g0, g1 = g[top, head(h)], g[low, head(h)]
-        gacc[top, head(h)] = nn(sup[h, 0], g0) + nn(sup[h, 1], g1)
+        g1 = g[low, head(h)]
+        gacc[top, head(h)] += nn(sup[h, 1], g1)
         gacc[low, head(h)] = nn(sup[h, 2], g1)
 
-    loop(4, 8, query_low)
-    ring_b1.relay(0)
-    ring_b1.relay(1)
+    loop(0, 8, query_low)
+    for r in range(2, 4):
+        rings[r].relay(0)
+        rings[r].relay(1)
     loop(8, 16, query_low)
-    loop(0, 4, key_scored)
     qd.send_down()
 
-    def stage_two(first, second, to):
-        first.wait_results()
-        for half in range(2):
-            part = first.result(half)
-            for i in range(2):
-                to[2 * half + i] = part[i].astype(BF).reshape(2, 64, 512)
+    def stage_two(firsts, second, to):
+        for n, first in enumerate(firsts):
+            first.wait_results()
+            for half in range(2):
+                part = first.result(half)
+                for i in range(2):
+                    to[2 * half + i, :, :, pl.ds(256 * n, 256)] = part[i].astype(BF).reshape(2, 64, 256)
         second.send_far()
         second.send_near(0)
         second.send_near(1)
 
-    loop(4, 8, key_scored)
-    stage_two(ring_a1, ring_a2, s1a)
+    loop(0, 8, key_scored)
     loop(8, 12, key_scored)
-    stage_two(ring_b1, ring_b2, s1b)
+    stage_two((rings[0], rings[2]), last_z, s1a)
+    stage_two((rings[1], rings[3]), last_y, s1b)
+    qd.send_back_x(None)
     loop(12, 16, key_scored)
-    qd.send_back_x(None)
-    ring_a2.relay(0)
-    ring_a2.relay(1)
-    loop(0, 4, value_scored)
-    ring_b2.relay(0)
-    ring_b2.relay(1)
-    loop(4, 12, value_scored)
+    loop(0, 8, value_scored)
+    last_z.relay(0)
+    last_z.relay(1)
+    last_y.relay(0)
+    last_y.relay(1)
+    loop(8, 16, value_scored)
     qd.send_back_core()
-    loop(12, 16, value_scored)
-    ring_a2.wait_results()
-    ring_b2.wait_results()
-    for i, ring in enumerate((ring_a2, ring_b2)):
+
+    def key_grad(h):
+        hs = head(h)
+        kg[:, hs] = (intra[h] + nt(v[:, hs], qd.st[h])).astype(BF)
+
+    def value_grad(h):
+        hs = head(h)
+        vg[:, hs] = (gacc[:, hs] + nn(k[:, hs], qd.st[h])).astype(BF)
+
+    def last(n, i):
+        r = (at.p + i) % 4
+        return remote(
+            fin.at[n, r], fin_land.at[n, at.p], fin_sem.at[0, n, i - 1], fin_sem.at[1, n, i - 1], at.group(r)
+        )
+
+    def send_last(n, ring):
+        ring.wait_results()
         for half in range(2):
             part = ring.result(half).astype(BF)
             for j in range(2):
-                fin[half * 2 + j, :, pl.ds(512 * i, 512)] = part[32 * j : 32 * j + 32]
-
-    def last(i):
-        r = (at.p + i) % 4
-        return remote(fin.at[r], fin_land.at[at.p], fin_sem.at[0, i - 1], fin_sem.at[1, i - 1], at.group(r))
-
-    for i in range(1, 4):
-        last(i).start()
-    fin_land[at.p] = fin[at.p]
+                fin[n, half * 2 + j] = part[32 * j : 32 * j + 32]
+        for i in range(1, 4):
+            last(n, i).start()
+        fin_land[n, at.p] = fin[n, at.p]
+
+    send_last(0, last_z)
+    loop(0, 8, lambda i: key_grad(8 * core + i))
+    send_last(1, last_y)
+    loop(0, 8, lambda i: value_grad(8 * core + i))
     qd.finish()
-
-    def key_grad(h):
-        hs = head(h)
-        kg[:, hs] = (intra[h] + nt(v[:, hs], qd.st[h])).astype(BF)
-
-    def value_grad(h):
-        hs = head(h)
-        vg[:, hs] = (gacc[:, hs] + nn(k[:, hs], qd.st[h])).astype(BF)
-
-    loop(0, 16, key_grad)
-    loop(0, 16, value_grad)
-    for i in range(1, 4):
-        last(i).wait()
+    loop(0, 8, lambda i: key_grad(8 * (1 - core) + i))
+    loop(0, 8, lambda i: value_grad(8 * (1 - core) + i))
+    for n in range(2):
+        for i in range(1, 4):
+            last(n, i).wait()
     for c in range(2):
-        r = fin_land[c].astype(F32) + fin_land[2 + c].astype(F32)
-        wg[:, pl.ds(pl.multiple_of(tp * 1024 + c * 512, 512), 512)] = r[:, :512]
-        wg[:, pl.ds(pl.multiple_of((1 - tp) * 1024 + c * 512, 512), 512)] = r[:, 512:]
-
-
-def scan_scratch():
-    piece = VM((16, 32, 128), F32)
+        for n in range(2):
+            total = fin_land[n, c].astype(F32) + fin_land[n, 2 + c].astype(F32)
+            for i in range(2):
+                start = (tp if i == 0 else 1 - tp) * 1024 + c * 512 + 256 * n
+                wg[:, pl.ds(pl.multiple_of(start, 256), 256)] = total[:, 256 * i : 256 * i + 256]
+
+
+def scan_scratch(kind):
+    piece = VM((16, 32, 128), kind)
     return (
         VM((16, 128, 128), BF),
         VM((8, 128, 128), BF),
         VM((2, 4, 128, 128), BF),
         VM((4, 128, 128), BF),
         piece, piece, piece, piece,
+        VM((4, 128, 128), F32),
         VM((4, 128, 128), BF),
         VM((4, 128, 128), BF),
         VM((8, 128, 128), BF),
@@ -514,11 +540,20 @@
     )
 
 
+def put_out(*refs):
+    sems = refs[8]
+    copies = [pltpu.make_async_copy(refs[i], refs[4 + i], sems.at[i]) for i in range(4)]
+    for copy in copies:
+        copy.start()
+    for copy in copies:
+        copy.wait()
+
+
 def local(queries, keys, values, cotangent, out_weight, memory):
     tok = VM((512, 2048), BF)
     any_spec = pl.BlockSpec(memory_space=pl.ANY)
     like = jax.ShapeDtypeStruct((512, 2048), BF)
-    return pl.pallas_call(
+    grads = pl.pallas_call(
         kernel,
         out_shape=(VM((512, 2048), BF), VM((512, 2048), BF), VM((512, 2048), BF), VM((32, 2048), F32)),
         in_specs=[any_spec] * 6,
@@ -532,31 +567,38 @@
             VM((512, 2048), F32),
             tok,
             VM((16, 512, 128), F32),
-            scan_scratch(),
-            scan_scratch(),
+            scan_scratch(F32),
+            scan_scratch(BF),
             VM((16, 3, 256, 256), BF),
+            VM((16, 128, 128), F32),
             VM((2, 4, 4, 128, 512), BF),
-            VM((4, 2, 2, 128, 512), BF),
-            VM((4, 2, 2, 128, 512), BF),
-            VM((2, 3, 2, 128, 512), BF),
-            VM((2, 3, 2, 128, 512), BF),
+            (VM((4, 2, 2, 128, 256), BF),) * 4,
+            (VM((2, 3, 2, 128, 256), BF),) * 4,
             VM((4, 2, 64, 512), BF),
             VM((4, 2, 64, 512), BF),
             VM((2, 3, 64, 512), BF),
             VM((2, 3, 64, 512), BF),
-            VM((4, 32, 1024), BF),
-            VM((4, 32, 1024), BF),
-            DMA((7,)),
+            VM((2, 4, 32, 512), BF),
+            VM((2, 4, 32, 512), BF),
+            DMA((15,)),
             DMA((2, 4)),
             DMA((2, 2)),
             DMA((2, 4)),
-            DMA((4, 2, 2, 3)),
-            DMA((2, 3)),
+            DMA((6, 2, 2, 3)),
+            DMA((2, 2, 3)),
         ],
         compiler_params=pltpu.CompilerParams(
             collective_id=0, has_side_effects=True, vmem_limit_bytes=59768832
         ),
     )(queries, keys, values, cotangent, out_weight, memory)
+    return pl.pallas_call(
+        put_out,
+        out_shape=(like, like, like, jax.ShapeDtypeStruct((32, 2048), F32)),
+        in_specs=[any_spec] * 4,
+        out_specs=(any_spec,) * 4,
+        scratch_shapes=[DMA((4,))],
+        compiler_params=pltpu.CompilerParams(vmem_limit_bytes=1048576),
+    )(*grads)
 
 
 def solution(mesh):

time: 90.6 us -> 83.9 us (0.926)
  local copies, waits for them, and re-layouts: 4.66 us -> 0 us
  Pallas kernels: 85.1 us -> 83 us
    pallas_call x1, Pallas kernels: 85.1 us -> 80.2 us  [local(): pl.pallas_call(kernel, out_shape=(VM((512, 2048), BF), VM((512, 2048), BF...]
    unnamed x4 -> x0, local copies, waits for them, and re-layouts: 4.66 us -> none
    pallas_call x0 -> x1, Pallas kernels: none -> 2.75 us  [local(): pl.pallas_call(put_out, out_shape=(like, like, like, jax.ShapeDtypeStruct...]
where the time goes in v3:
time: 83.9 us; the launch traced here: 83.8 us
  Pallas kernels  83 us (99%)
    pallas_call x1, Pallas kernels, local(): pl.pallas_call(kernel, out_shape=(VM((512, 2048), BF), VM((512, 2048), BF...  80.2 us
    pallas_call x1, Pallas kernels, local(): pl.pallas_call(put_out, out_shape=(like, like, like, jax.ShapeDtypeStruct...  2.75 us

profile of v3, /device:TPU:1, one launch (start us, length us, event | category | flops | bytes accessed | tf_op | source)
XLA Modules:
  0.0 83.8 jit_solution(17512084521493210559)
XLA Ops:
  0.6 80.2 %shard_map.93 = (bf16[512,2048]{1,0:T(8,128)(2,1)S(1)}, bf16[512,2048]{1,0:T(8,128)(2,1)S(1)}, bf16[512,2048]{1,0:T(8,128)(2,1)S(1)}, f32[32,2048]{1,0:T(8,128)S(1)}) custom-call(bf16[512,2048]{1,0:T(8,128)(2,1)} %q_hbm.1, bf16[512,2048]{1,0:T(8,128)(2,1)} %k_hbm.1, bf16[512,2048]{1,0:T(8,128)(2,1)} %v_hbm.1, bf16[512,1024]{1,0:T(8,128)(2,1)} %cot_hbm.1, ...), custom_call_target="tpu_custom_call" | custom-call | tf_op jit(solution)/shard_map/pallas_call | solution.py:556
  80.9 2.8 %shard_map.94 = (bf16[512,2048]{1,0:T(8,128)(2,1)}, bf16[512,2048]{1,0:T(8,128)(2,1)}, bf16[512,2048]{1,0:T(8,128)(2,1)}, f32[32,2048]{1,0:T(8,128)}) custom-call(bf16[512,2048]{1,0:T(8,128)(2,1)S(1)} %get-tuple-element.8.refs_0_, bf16[512,2048]{1,0:T(8,128)(2,1)S(1)} %get-tuple-element.9.refs_1_, bf16[512,2048]{1,0:T(8,128)(2,1)S(1)} %get-tuple-element.10.refs_2_, ...), custom_call_target="tpu_custom_call" | custom-call | tf_op jit(solution)/shard_map/pallas_call | solution.py:594

commit v4 on v3

--- a/solution.py
+++ b/solution.py
@@ -256,7 +256,7 @@
 
     cot_copies = [
         remote(cot_hbm.at[rows], cot.at[tp, rows], tp_sem.at[0, i], tp_sem.at[1, i], peer_tp)
-        for i, rows in enumerate((pl.ds(0, 64), pl.ds(64, 192), pl.ds(256, 64), pl.ds(320, 192)))
+        for i, rows in enumerate((pl.ds(0, 64), pl.ds(64, 192), pl.ds(256, 64), pl.ds(320, 96), pl.ds(416, 96)))
     ]
     near_cot = remote(cot_hbm.at[:, mine(1 - core)], pcot.at[0], pc_sem.at[0, 0], pc_sem.at[1, 0], peer_core)
     far_cot = remote(cot.at[1 - tp, :, mine(1 - core)], pcot.at[1], pc_sem.at[0, 1], pc_sem.at[1, 1], peer_core)
@@ -325,8 +325,9 @@
         gacc[:, wrows(n)] = nt(cot[tp], w[tp, wrows(n), :])
 
     each(0, 8, grad_own)
-    loop(0, 8, turned)
+    loop(0, 4, turned)
     kv.send_down()
+    loop(4, 16, turned)
 
     def grad_top(n):
         g[top, wrows(n)] = (gacc[top, wrows(n)] + nt(cot[1 - tp, top, :], w[1 - tp, wrows(n), :])).astype(BF)
@@ -335,12 +336,12 @@
         g[low, wrows(n)] = (gacc[low, wrows(n)] + nt(cot[1 - tp, low, :], w[1 - tp, wrows(n), :])).astype(BF)
 
     loads[4].wait()
-    loop(8, 16, turned)
     cot_copies[0].wait()
     cot_copies[1].wait()
-    each(0, 8, grad_top)
+    each(0, 4, grad_top)
     kv.send_back_x(mem)
     cot_copies[3].start()
+    each(4, 8, grad_top)
 
     def top_rows(h):
         hs = head(h)
@@ -351,6 +352,7 @@
 
     loop(0, 16, top_rows)
     kv.send_back_core()
+    cot_copies[4].start()
     kv.finish()
 
     def attend(h):
@@ -402,39 +404,40 @@
         part(r, 2)
         rings[r].send_far()
     for r in range(2):
-        part(r, 1)
-        rings[r].send_near(0)
-    cot_copies[2].wait()
-    cot_copies[3].wait()
+        for way, i in ((0, 1), (1, 3)):
+            part(r, i)
+            rings[r].send_near(way)
+    for copy in cot_copies[2:]:
+        copy.wait()
     far_cot.start()
     each(0, 8, grad_low)
+    for r in range(2):
+        rings[r].relay(0)
+        rings[r].relay(1)
 
     def qd_sum(h):
         qd.s[h] = (qacc[h] + tn(q[low, head(h)], g[low, head(h)])).astype(BF)
 
     loop(0, 16, qd_sum)
     qd.send_core()
-    for r in range(2):
-        part(r, 3)
-        rings[r].send_near(1)
-    qd.send_x()
     far_cot.wait()
     for r in range(2, 4):
         part(r, 2)
         rings[r].send_far()
-    for r in range(2):
+    part(2, 1)
+    rings[2].send_near(0)
+    qd.send_x()
+    for r, way, i in ((2, 1, 3), (3, 0, 1), (3, 1, 3)):
+        part(r, i)
+        rings[r].send_near(way)
+    for r in range(4):
+        part(r, 0)
+    loop(0, 8, query_low)
+    qd.send_up()
+    for r in range(2, 4):
         rings[r].relay(0)
         rings[r].relay(1)
-        part(r, 0)
-    for r in range(2, 4):
-        for i in (1, 3):
-            part(r, i)
-    qd.send_up()
-    for r in range(2, 4):
-        rings[r].send_near(0)
-        rings[r].send_near(1)
-    for r in range(2, 4):
-        part(r, 0)
+    loop(8, 16, query_low)
 
     def key_scored(h):
         hs = head(h)
@@ -446,13 +449,6 @@
         g1 = g[low, head(h)]
         gacc[top, head(h)] += nn(sup[h, 1], g1)
         gacc[low, head(h)] = nn(sup[h, 2], g1)
-
-    loop(0, 8, query_low)
-    for r in range(2, 4):
-        rings[r].relay(0)
-        rings[r].relay(1)
-    loop(8, 16, query_low)
-    qd.send_down()
 
     def stage_two(firsts, second, to):
         for n, first in enumerate(firsts):
@@ -465,19 +461,19 @@
         second.send_near(0)
         second.send_near(1)
 
-    loop(0, 8, key_scored)
-    loop(8, 12, key_scored)
+    loop(0, 4, key_scored)
+    qd.send_down()
+    loop(4, 8, key_scored)
     stage_two((rings[0], rings[2]), last_z, s1a)
     stage_two((rings[1], rings[3]), last_y, s1b)
+    loop(8, 16, key_scored)
+    loop(0, 8, value_scored)
     qd.send_back_x(None)
-    loop(12, 16, key_scored)
-    loop(0, 8, value_scored)
     last_z.relay(0)
     last_z.relay(1)
     last_y.relay(0)
     last_y.relay(1)
     loop(8, 16, value_scored)
-    qd.send_back_core()
 
     def key_grad(h):
         hs = head(h)
@@ -504,8 +500,9 @@
         fin_land[n, at.p] = fin[n, at.p]
 
     send_last(0, last_z)
+    send_last(1, last_y)
+    qd.send_back_core()
     loop(0, 8, lambda i: key_grad(8 * core + i))
-    send_last(1, last_y)
     loop(0, 8, lambda i: value_grad(8 * core + i))
     qd.finish()
     loop(0, 8, lambda i: key_grad(8 * (1 - core) + i))
@@ -581,7 +578,7 @@
             VM((2, 4, 32, 512), BF),
             VM((2, 4, 32, 512), BF),
             DMA((15,)),
-            DMA((2, 4)),
+            DMA((2, 5)),
             DMA((2, 2)),
             DMA((2, 4)),
             DMA((6, 2, 2, 3)),

time: 83.9 us -> 79.2 us (0.944)
  Pallas kernels: 83 us -> 78.3 us
    pallas_call x1, Pallas kernels: 80.2 us -> 75.5 us  [local(): pl.pallas_call(kernel, out_shape=(VM((512, 2048), BF), VM((512, 2048), BF...]
where the time goes in v4:
time: 79.2 us; the launch traced here: 79.1 us
  Pallas kernels  78.3 us (99%)
  between operations  0.8 us (1%)
    pallas_call x1, Pallas kernels, local(): pl.pallas_call(kernel, out_shape=(VM((512, 2048), BF), VM((512, 2048), BF...  75.5 us
    pallas_call x1, Pallas kernels, local(): pl.pallas_call(put_out, out_shape=(like, like, like, jax.ShapeDtypeStruct...  2.75 us

profile of v4, /device:TPU:1, one launch (start us, length us, event | category | flops | bytes accessed | tf_op | source)
XLA Modules:
  0.0 79.1 jit_solution(8659326669314547723)
XLA Ops:
  0.6 75.5 %shard_map.93 = (bf16[512,2048]{1,0:T(8,128)(2,1)S(1)}, bf16[512,2048]{1,0:T(8,128)(2,1)S(1)}, bf16[512,2048]{1,0:T(8,128)(2,1)S(1)}, f32[32,2048]{1,0:T(8,128)S(1)}) custom-call(bf16[512,2048]{1,0:T(8,128)(2,1)} %q_hbm.1, bf16[512,2048]{1,0:T(8,128)(2,1)} %k_hbm.1, bf16[512,2048]{1,0:T(8,128)(2,1)} %v_hbm.1, bf16[512,1024]{1,0:T(8,128)(2,1)} %cot_hbm.1, ...), custom_call_target="tpu_custom_call" | custom-call | tf_op jit(solution)/shard_map/pallas_call | solution.py:553
  76.2 2.8 %shard_map.94 = (bf16[512,2048]{1,0:T(8,128)(2,1)}, bf16[512,2048]{1,0:T(8,128)(2,1)}, bf16[512,2048]{1,0:T(8,128)(2,1)}, f32[32,2048]{1,0:T(8,128)}) custom-call(bf16[512,2048]{1,0:T(8,128)(2,1)S(1)} %get-tuple-element.8.refs_0_, bf16[512,2048]{1,0:T(8,128)(2,1)S(1)} %get-tuple-element.9.refs_1_, bf16[512,2048]{1,0:T(8,128)(2,1)S(1)} %get-tuple-element.10.refs_2_, ...), custom_call_target="tpu_custom_call" | custom-call | tf_op jit(solution)/shard_map/pallas_call | solution.py:591

commit v5 on v4

--- a/solution.py
+++ b/solution.py
@@ -407,6 +407,8 @@
         for way, i in ((0, 1), (1, 3)):
             part(r, i)
             rings[r].send_near(way)
+    for r in range(2):
+        part(r, 0)
     for copy in cot_copies[2:]:
         copy.wait()
     far_cot.start()
@@ -430,7 +432,7 @@
     for r, way, i in ((2, 1, 3), (3, 0, 1), (3, 1, 3)):
         part(r, i)
         rings[r].send_near(way)
-    for r in range(4):
+    for r in range(2, 4):
         part(r, 0)
     loop(0, 8, query_low)
     qd.send_up()
@@ -463,10 +465,9 @@
 
     loop(0, 4, key_scored)
     qd.send_down()
-    loop(4, 8, key_scored)
     stage_two((rings[0], rings[2]), last_z, s1a)
     stage_two((rings[1], rings[3]), last_y, s1b)
-    loop(8, 16, key_scored)
+    loop(4, 16, key_scored)
     loop(0, 8, value_scored)
     qd.send_back_x(None)
     last_z.relay(0)
@@ -539,7 +540,11 @@
 
 def put_out(*refs):
     sems = refs[8]
-    copies = [pltpu.make_async_copy(refs[i], refs[4 + i], sems.at[i]) for i in range(4)]
+    copies = [pltpu.make_async_copy(refs[3], refs[7], sems.at[0])]
+    for i in range(3):
+        for j in range(4):
+            rows = pl.ds(128 * j, 128)
+            copies.append(pltpu.make_async_copy(refs[i].at[rows], refs[4 + i].at[rows], sems.at[1 + 4 * i + j]))
     for copy in copies:
         copy.start()
     for copy in copies:
@@ -593,7 +598,7 @@
         out_shape=(like, like, like, jax.ShapeDtypeStruct((32, 2048), F32)),
         in_specs=[any_spec] * 4,
         out_specs=(any_spec,) * 4,
-        scratch_shapes=[DMA((4,))],
+        scratch_shapes=[DMA((13,))],
         compiler_params=pltpu.CompilerParams(vmem_limit_bytes=1048576),
     )(*grads)
 

time: 79.2 us -> 80.3 us (1.014)
  Pallas kernels: 78.3 us -> 79.4 us
    pallas_call x1, Pallas kernels: 75.5 us -> 76.5 us  [local(): pl.pallas_call(kernel, out_shape=(VM((512, 2048), BF), VM((512, 2048), BF...]
where the time goes in v5:
time: 80.3 us; the launch traced here: 80.2 us
  Pallas kernels  79.4 us (99%)
    pallas_call x1, Pallas kernels, local(): pl.pallas_call(kernel, out_shape=(VM((512, 2048), BF), VM((512, 2048), BF...  76.5 us
    pallas_call x1, Pallas kernels, local(): pl.pallas_call(put_out, out_shape=(like, like, like, jax.ShapeDtypeStruct...  2.85 us

profile of v5, /device:TPU:1, one launch (start us, length us, event | category | flops | bytes accessed | tf_op | source)
XLA Modules:
  0.0 80.2 jit_solution(17770430520574466726)
XLA Ops:
  0.6 76.5 %shard_map.93 = (bf16[512,2048]{1,0:T(8,128)(2,1)S(1)}, bf16[512,2048]{1,0:T(8,128)(2,1)S(1)}, bf16[512,2048]{1,0:T(8,128)(2,1)S(1)}, f32[32,2048]{1,0:T(8,128)S(1)}) custom-call(bf16[512,2048]{1,0:T(8,128)(2,1)} %q_hbm.1, bf16[512,2048]{1,0:T(8,128)(2,1)} %k_hbm.1, bf16[512,2048]{1,0:T(8,128)(2,1)} %v_hbm.1, bf16[512,1024]{1,0:T(8,128)(2,1)} %cot_hbm.1, ...), custom_call_target="tpu_custom_call" | custom-call | tf_op jit(solution)/shard_map/pallas_call | solution.py:558
  77.1 2.8 %shard_map.94 = (bf16[512,2048]{1,0:T(8,128)(2,1)}, bf16[512,2048]{1,0:T(8,128)(2,1)}, bf16[512,2048]{1,0:T(8,128)(2,1)}, f32[32,2048]{1,0:T(8,128)}) custom-call(bf16[512,2048]{1,0:T(8,128)(2,1)S(1)} %get-tuple-element.8.refs_0_, bf16[512,2048]{1,0:T(8,128)(2,1)S(1)} %get-tuple-element.9.refs_1_, bf16[512,2048]{1,0:T(8,128)(2,1)S(1)} %get-tuple-element.10.refs_2_, ...), custom_call_target="tpu_custom_call" | custom-call | tf_op jit(solution)/shard_map/pallas_call | solution.py:596
